TPU v7x, 256 devices: a whole 4x4x8 slice. The times are simulated.
256 devices in a mesh: seq: 128 (over z, y_hi, x, core), head: 2 (over y_lo).
Axes of the slice: x: 4, y: 4 (y_hi: 2, y_lo: 2; y = y_hi * 2 + y_lo), z: 8, core: 2. Of those that a mesh axis runs over, the one named last changes fastest.
Arguments:
- queries: bfloat16 [16384, 2048], P(('seq', 'head')), may hold values from -8 to 8
- key_rows: bfloat16 [16384, 2048], P(('seq', 'head')), may hold values from -8 to 8
- values: bfloat16 [16384, 2048], P(('seq', 'head')), may hold values from -6 to 6
- out_grad: bfloat16 [16384, 2048], P(('seq', 'head')), may hold values from -6 to 6
Outputs:
- attended: bfloat16 [16384, 2048], P(('seq', 'head'))
- query_grad: bfloat16 [16384, 2048], P(('seq', 'head'))
- key_grad: bfloat16 [16384, 2048], P(('seq', 'head'))
- value_grad: bfloat16 [16384, 2048], P(('seq', 'head'))
All inputs are finite; a program needn't handle non-finite values.
Results may differ from a plain program's by a relative error of at most 0.028.
Values may be sent and summed in bfloat16 or wider, within the bound.
A program may use at most 64 MiB of HBM per device.

v0:
```python
import math
import jax
import jax.numpy as jnp
from jax import lax
from jax.sharding import PartitionSpec as P

HEAD_DIM = 128
ROOT_HALF = 0.7071067811865476


def swapped(block, axis, distance):
    count = lax.axis_size(axis)
    route = []
    for low in range(count):
        high = low | 1 << distance
        if high != low and high < count:
            route += [(low, high), (high, low)]
    return lax.ppermute(block, axis, route)


def pool_rows(blocks):
    widened = blocks.astype(jnp.float32)
    paired = widened.reshape((widened.shape[0] // 2, 2) + widened.shape[1:])
    return ((paired[:, 0] + paired[:, 1]) * ROOT_HALF).astype(jnp.bfloat16)


def unpool_rows(blocks):
    return jnp.repeat(blocks, 2, axis=0) * ROOT_HALF


def local(queries, key_rows, values, out_grad):
    query_in, key_in, value_in, grad_in = (
        lax.all_to_all(queries, "head", split_axis=1, concat_axis=0, tiled=True),
        lax.all_to_all(key_rows, "head", split_axis=1, concat_axis=0, tiled=True),
        lax.all_to_all(values, "head", split_axis=1, concat_axis=0, tiled=True),
        lax.all_to_all(out_grad, "head", split_axis=1, concat_axis=0, tiled=True),
    )
    token_rows = query_in.shape[0]
    head_count = query_in.shape[1] // HEAD_DIM
    local_shape = (token_rows, head_count, HEAD_DIM)
    query_loc = query_in.reshape(local_shape)
    key_loc = key_in.reshape(local_shape)
    value_loc = value_in.reshape(local_shape)
    grad_loc = grad_in.reshape(local_shape)
    level_count = lax.axis_size("seq").bit_length() - 1
    seq_index = lax.axis_index("seq")
    half_rows = token_rows // 2
    scale_factor = 1.0 / math.sqrt(HEAD_DIM)
    top_bit = seq_index >> level_count - 1 & 1
    sibling_start = (1 - top_bit) * half_rows
    query_pool = [query_loc]
    key_pool = [key_loc]
    value_pool = [value_loc]
    for level_no in range(1, level_count + 1):
        query_pool.append(pool_rows(query_pool[-1]))
        key_pool.append(pool_rows(key_pool[-1]))
        value_pool.append(pool_rows(value_pool[-1]))
    own_keys = key_pool[1]
    own_values = value_pool[1]
    records = []
    for level_no in range(1, level_count + 1):
        if level_no < level_count:
            sib_keys, sib_values = swapped((own_keys, own_values), "seq", level_no - 1)
        else:
            whole_keys, whole_values = (
                lax.all_gather(key_pool[level_count], "seq", axis=0, tiled=True),
                lax.all_gather(value_pool[level_count], "seq", axis=0, tiled=True),
            )
            sib_keys = lax.dynamic_slice_in_dim(whole_keys, sibling_start, half_rows, 0)
            sib_values = lax.dynamic_slice_in_dim(whole_values, sibling_start, half_rows, 0)
        coarse_scores = (
            jnp.einsum(
                "ghd,chd->ghc", query_pool[level_no], sib_keys, preferred_element_type=jnp.float32
            )
            * scale_factor
        )
        coarse_top = jnp.max(coarse_scores, axis=-1)
        coarse_expo = jnp.exp(coarse_scores - coarse_top[..., None])
        coarse_total = jnp.sum(coarse_expo, axis=-1)
        expo_half = coarse_expo.astype(jnp.bfloat16)
        coarse_numer = jnp.einsum(
            "ghc,chd->ghd", expo_half, sib_values, preferred_element_type=jnp.float32
        )
        records.append(
            (sib_keys, sib_values, coarse_expo, expo_half, coarse_top, coarse_total, coarse_numer)
        )
        if level_no < level_count - 1:
            own_bit = seq_index >> level_no - 1 & 1
            lower_keys = jnp.where(own_bit == 0, own_keys, sib_keys)
            upper_keys = jnp.where(own_bit == 0, sib_keys, own_keys)
            lower_values = jnp.where(own_bit == 0, own_values, sib_values)
            upper_values = jnp.where(own_bit == 0, sib_values, own_values)
            own_keys = pool_rows(jnp.concatenate([lower_keys, upper_keys], axis=0))
            own_values = pool_rows(jnp.concatenate([lower_values, upper_values], axis=0))
    local_scores = (
        jnp.einsum("thd,uhd->thu", query_loc, key_loc, preferred_element_type=jnp.float32)
        * scale_factor
    )
    row_top = jnp.max(local_scores, axis=-1)
    for level_no in range(1, level_count + 1):
        row_top = jnp.maximum(row_top, jnp.repeat(records[level_no - 1][4], 2**level_no, axis=0))
    local_expo = jnp.exp(local_scores - row_top[..., None])
    row_total = jnp.sum(local_expo, axis=-1)
    numer_all = jnp.einsum(
        "thu,uhd->thd",
        local_expo.astype(jnp.bfloat16),
        value_loc,
        preferred_element_type=jnp.float32,
    )
    factors = []
    for level_no in range(1, level_count + 1):
        group_rows = 2**level_no
        record = records[level_no - 1]
        factor = jnp.exp(jnp.repeat(record[4], group_rows, axis=0) - row_top)
        row_total = row_total + factor * jnp.repeat(record[5], group_rows, axis=0)
        numer_all = numer_all + factor[..., None] * jnp.repeat(record[6], group_rows, axis=0)
        factors.append(factor)
    outcome = numer_all / row_total[..., None]
    attended = outcome.astype(jnp.bfloat16).reshape(token_rows, -1)
    grad_wide = grad_loc.astype(jnp.float32)
    row_dots = jnp.sum(grad_wide * outcome, axis=-1)
    local_probs = local_expo / row_total[..., None]
    local_dprob = jnp.einsum(
        "thd,uhd->thu", grad_loc, value_loc, preferred_element_type=jnp.float32
    )
    dlocal = (local_probs * (local_dprob - row_dots[..., None])).astype(jnp.bfloat16)
    query_acc = (
        jnp.einsum("thu,uhd->thd", dlocal, key_loc, preferred_element_type=jnp.float32)
        * scale_factor
    )
    key_acc = (
        jnp.einsum("thu,thd->uhd", dlocal, query_loc, preferred_element_type=jnp.float32)
        * scale_factor
    )
    value_acc = jnp.einsum(
        "thu,thd->uhd",
        local_probs.astype(jnp.bfloat16),
        grad_loc,
        preferred_element_type=jnp.float32,
    )
    level_grads = []
    for level_no in range(1, level_count + 1):
        sib_keys, sib_values, coarse_expo, expo_half = records[level_no - 1][:4]
        group_rows = 2**level_no
        coarse_rows = token_rows // group_rows
        weight = factors[level_no - 1] / row_total
        adjoint = (
            (weight[..., None] * grad_wide)
            .reshape(coarse_rows, group_rows, head_count, HEAD_DIM)
            .sum(axis=1)
            .astype(jnp.bfloat16)
        )
        offset = (weight * row_dots).reshape(coarse_rows, group_rows, head_count).sum(axis=1)
        inner_dot = (
            jnp.einsum("ghd,chd->ghc", adjoint, sib_values, preferred_element_type=jnp.float32)
            - offset[..., None]
        )
        dcoarse = (coarse_expo * inner_dot).astype(jnp.bfloat16)
        dquery_level = (
            jnp.einsum("ghc,chd->ghd", dcoarse, sib_keys, preferred_element_type=jnp.float32)
            * scale_factor
        )
        dkey_sib = (
            jnp.einsum(
                "ghc,ghd->chd", dcoarse, query_pool[level_no], preferred_element_type=jnp.float32
            )
            * scale_factor
        )
        dvalue_sib = jnp.einsum(
            "ghc,ghd->chd", expo_half, adjoint, preferred_element_type=jnp.float32
        )
        level_grads.append((dquery_level, dkey_sib, dvalue_sib))
    query_carry = jnp.zeros((token_rows >> level_count, head_count, HEAD_DIM), jnp.float32)
    for level_no in range(level_count, 0, -1):
        query_carry = unpool_rows(query_carry + level_grads[level_no - 1][0])
    query_total = query_acc + query_carry
    tail_keys = None
    tail_values = None
    own_grad_keys = None
    own_grad_values = None
    spread_keys = jnp.zeros(local_shape, jnp.float32)
    spread_values = jnp.zeros(local_shape, jnp.float32)
    spread_keys = lax.dynamic_update_slice_in_dim(spread_keys, level_grads[-1][1], sibling_start, 0)
    spread_values = lax.dynamic_update_slice_in_dim(
        spread_values, level_grads[-1][2], sibling_start, 0
    )
    tail_keys, tail_values = (
        lax.psum_scatter(spread_keys, "seq", scatter_dimension=0, tiled=True),
        lax.psum_scatter(spread_values, "seq", scatter_dimension=0, tiled=True),
    )
    for level_no in range(level_count - 1, 0, -1):
        send_keys = level_grads[level_no - 1][1]
        send_values = level_grads[level_no - 1][2]
        keep_keys = None
        keep_values = None
        if own_grad_keys is not None:
            own_bit = seq_index >> level_no - 1 & 1
            wide_keys = unpool_rows(own_grad_keys)
            wide_values = unpool_rows(own_grad_values)
            keep_keys = jnp.where(own_bit == 0, wide_keys[:half_rows], wide_keys[half_rows:])
            keep_values = jnp.where(own_bit == 0, wide_values[:half_rows], wide_values[half_rows:])
            send_keys = send_keys + jnp.where(
                own_bit == 0, wide_keys[half_rows:], wide_keys[:half_rows]
            )
            send_values = send_values + jnp.where(
                own_bit == 0, wide_values[half_rows:], wide_values[:half_rows]
            )
        recv_keys, recv_values = (
            swapped(send_keys.astype(jnp.bfloat16), "seq", level_no - 1).astype(send_keys.dtype),
            swapped(send_values.astype(jnp.bfloat16), "seq", level_no - 1).astype(
                send_values.dtype
            ),
        )
        if keep_keys is None:
            own_grad_keys = recv_keys
            own_grad_values = recv_values
        else:
            own_grad_keys = keep_keys + recv_keys
            own_grad_values = keep_values + recv_values
    for level_no in range(level_count, 1, -1):
        tail_keys = unpool_rows(tail_keys)
        tail_values = unpool_rows(tail_values)
    base_keys = tail_keys
    base_values = tail_values
    base_keys = base_keys + own_grad_keys
    base_values = base_values + own_grad_values
    key_total = key_acc + unpool_rows(base_keys)
    value_total = value_acc + unpool_rows(base_values)
    query_out = query_total.astype(jnp.bfloat16).reshape(token_rows, -1)
    key_out = key_total.astype(jnp.bfloat16).reshape(token_rows, -1)
    value_out = value_total.astype(jnp.bfloat16).reshape(token_rows, -1)
    return (
        lax.all_to_all(attended, "head", split_axis=0, concat_axis=1, tiled=True),
        lax.all_to_all(query_out, "head", split_axis=0, concat_axis=1, tiled=True),
        lax.all_to_all(key_out, "head", split_axis=0, concat_axis=1, tiled=True),
        lax.all_to_all(value_out, "head", split_axis=0, concat_axis=1, tiled=True),
    )


def solution(mesh):
    in_specs = (
        P(("seq", "head"), None),
        P(("seq", "head"), None),
        P(("seq", "head"), None),
        P(("seq", "head"), None),
    )
    out_specs = (
        P(("seq", "head"), None),
        P(("seq", "head"), None),
        P(("seq", "head"), None),
        P(("seq", "head"), None),
    )
    return jax.shard_map(local, mesh=mesh, in_specs=in_specs, out_specs=out_specs, check_vma=False)
```

profile of v0, /device:TPU:8, one launch (start us, length us, event | category | flops | bytes accessed | tf_op | source)
XLA Modules:
  0.0 1857.8 jit_solution(11937206118050483747)
XLA Ops:
  7.2 1.7 copy.2307
  8.8 5.7 all-to-all-start.1
  18.7 4.5 all-to-all-start
  24.6 1.8 all-to-all-done
  26.4 5.4 all-to-all-start.2
  35.5 4.9 all-to-all-start.4
  42.0 184.1 %all-gather = bf16[128,1,8,128]{3,2,1,0:T(8,128)(2,1)S(1)} all-gather(bf16[1,1,8,128]{3,2,1,0:T(8,128)(2,1)S(1)} %fusion.264), channel_id=2, replica_groups=mesh['seq'=128,'head'=2] {'seq'}, dimensions={0}, use_global_device_ids=true | all-gather | bytes 264192 | tf_op jit(solution)/shard_map/all_gather | solution.py:66
  226.7 175.9 %all-gather.1 = bf16[128,1,8,128]{3,2,1,0:T(8,128)(2,1)S(1)} all-gather(bf16[1,1,8,128]{3,2,1,0:T(8,128)(2,1)S(1)} %fusion.260), channel_id=3, replica_groups=mesh['seq'=128,'head'=2] {'seq'}, dimensions={0}, use_global_device_ids=true | all-gather | bytes 264192 | tf_op jit(solution)/shard_map/all_gather | solution.py:67
  410.0 1.8 collective-permute-start.1
  430.3 3.5 collective-permute-start.8
  452.2 3.6 collective-permute-start.9
  467.4 2.1 collective-permute-start.10
  482.6 3.2 collective-permute-start.11
  498.4 1.4 fusion.281
  501.2 3.7 multiply_reduce_fusion.4
  534.5 2.2 collective-permute-start.12
  549.8 4.8 all-to-all-start.5
  561.8 2.3 collective-permute-start.13
  568.3 2.6 collective-permute-start.14
  571.0 1.7 collective-permute-done.20
  576.1 2.7 collective-permute-start.15
  578.8 1.8 collective-permute-done.21
  581.2 3.0 collective-permute-start.22
  585.6 1.5 collective-permute-done.22
  587.7 2.1 collective-permute-done.16
  590.3 1227.6 %all-reduce.5.cloned.1.call-done = (f32[128,8,128]{2,1,0:T(8,128)}, f32[128,8,128]{2,1,0:T(8,128)}) async-done(((f32[128,8,128]{2,1,0:T(8,128)}, f32[128,8,128]{2,1,0:T(8,128)}), (f32[128,8,128]{2,1,0:T(8,128)}, f32[128,8,128]{2,1,0:T(8,128)})) %all-reduce.5.cloned.1.call-update) | async-done | bytes 1048592
  1822.9 4.9 all-to-all-start.3
  1827.9 4.1 all-to-all-done.3
  1832.1 5.6 all-to-all-start.7
  1839.1 2.6 all-to-all-done.7
  1841.7 5.2 all-to-all-start.6
  1846.9 1.7 copy.1949
  (888 shorter events, 160.8 us)
Async XLA Ops:
  8.8 9.9 all-to-all-start.1
  18.7 7.7 all-to-all-start
  26.4 9.1 all-to-all-start.2
  34.8 374.6 %collective-permute-start = (bf16[64,8,128]{2,0,1:T(8,128)(2,1)S(1)}, bf16[64,8,128]{2,0,1:T(8,128)(2,1)S(1)}, u32[]{:S(2)}, u32[]{:S(2)}) collective-permute-start(bf16[64,8,128]{2,0,1:T(8,128)(2,1)S(1)} %bitcast.781), channel_id=1, source_target_pairs={{0,2},{2,0},{4,6},{6,4},{8,10},{10,8},{12,14},{14,12},{16,18},{18,... | collective-permute-start | bytes 393224 | tf_op jit(solution)/shard_map/ppermute | solution.py:18
  35.5 368.7 %all-to-all-start.4 = ((bf16[64,2,1024]{2,0,1:T(8,128)(2,1)}), bf16[64,2,1024]{2,0,1:T(8,128)(2,1)S(1)}, u32[]{:S(2)}, u32[]{:S(2)}) async-start(bf16[64,2,1024]{2,0,1:T(8,128)(2,1)} %bitcast.706), calls=%async_computation.4 | async-start | bytes 524288 | tf_op jit(solution)/shard_map/all_to_all | solution.py:36
  40.7 368.7 %collective-permute-start.6 = (bf16[64,8,128]{2,0,1:T(8,128)(2,1)S(1)}, bf16[64,8,128]{2,0,1:T(8,128)(2,1)S(1)}, u32[]{:S(2)}, u32[]{:S(2)}) collective-permute-start(bf16[64,8,128]{2,0,1:T(8,128)(2,1)S(1)} %bitcast.783), channel_id=1, source_target_pairs={{0,2},{2,0},{4,6},{6,4},{8,10},{10,8},{12,14},{14,12},{16,18},{18,... | collective-permute-start | bytes 393224 | tf_op jit(solution)/shard_map/ppermute | solution.py:18
  410.0 13.9 collective-permute-start.1
  416.0 12.2 collective-permute-start.7
  424.5 16.9 collective-permute-start.2
  430.3 19.1 %collective-permute-start.8 = (bf16[64,8,128]{2,0,1:T(8,128)(2,1)}, bf16[64,8,128]{2,0,1:T(8,128)(2,1)S(1)}, u32[]{:S(2)}, u32[]{:S(2)}) collective-permute-start(bf16[64,8,128]{2,0,1:T(8,128)(2,1)} %fusion.136), channel_id=1, source_target_pairs={{0,8},{8,0},{2,10},{10,2},{4,12},{12,4},{6,14},{14,6},{16,24},{24,... | collective-permute-start | bytes 393224 | tf_op jit(solution)/shard_map/ppermute | solution.py:18
  449.4 9.1 collective-permute-start.3
  452.2 13.2 collective-permute-start.9
  465.4 8.3 collective-permute-start.4
  467.4 12.0 collective-permute-start.10
  479.4 11.3 collective-permute-start.5
  482.6 12.5 collective-permute-start.11
  520.3 37.5 %collective-permute-start.18 = (bf16[64,8,128]{2,0,1:T(8,128)(2,1)}, bf16[64,8,128]{2,0,1:T(8,128)(2,1)}, u32[]{:S(2)}, u32[]{:S(2)}) collective-permute-start(bf16[64,8,128]{2,0,1:T(8,128)(2,1)} %fusion.60), channel_id=1, source_target_pairs={{0,64},{64,0},{2,66},{66,2},{4,68},{68,4},{6,70},{70,6},{8,72},{72... | collective-permute-start | bytes 393224 | tf_op jit(solution)/shard_map/ppermute | solution.py:18
  534.5 25.4 %collective-permute-start.12 = (bf16[64,8,128]{2,0,1:T(8,128)(2,1)}, bf16[64,8,128]{2,0,1:T(8,128)(2,1)}, u32[]{:S(2)}, u32[]{:S(2)}) collective-permute-start(bf16[64,8,128]{2,0,1:T(8,128)(2,1)} %fusion.53), channel_id=1, source_target_pairs={{0,64},{64,0},{2,66},{66,2},{4,68},{68,4},{6,70},{70,6},{8,72},{72... | collective-permute-start | bytes 393224 | tf_op jit(solution)/shard_map/ppermute | solution.py:18
  549.8 1273.1 %all-to-all-start.5 = ((bf16[2,64,1024]{2,1,0:T(8,128)(2,1)}), bf16[2,64,1024]{2,1,0:T(8,128)(2,1)}, u32[]{:S(2)}, u32[]{:S(2)}) async-start(bf16[2,64,1024]{2,1,0:T(8,128)(2,1)} %all_to_all.120), calls=%async_computation.5 | async-start | bytes 524288 | tf_op jit(solution)/shard_map/all_to_all | solution.py:234
  554.7 1263.3 %all-reduce.5.cloned.1.call-start = ((), (), s32[]{:S(2)}) async-start(), calls=%async_computation.8 | async-start | bytes 2097152
  561.8 5.3 collective-permute-start.13
  566.1 6.6 collective-permute-start.20
  568.3 6.6 collective-permute-start.14
  573.9 6.7 collective-permute-start.21
  576.1 8.1 collective-permute-start.15
  581.2 5.9 collective-permute-start.22
  584.7 5.1 collective-permute-start.16
  587.6 1231.6 %collective-permute-start.23 = (bf16[64,8,128]{2,0,1:T(8,128)(2,1)S(1)}, bf16[64,8,128]{2,0,1:T(8,128)(2,1)S(1)}, u32[]{:S(2)}, u32[]{:S(2)}) collective-permute-start(bf16[64,8,128]{2,0,1:T(8,128)(2,1)S(1)} %fusion.46), channel_id=1, source_target_pairs={{0,2},{2,0},{4,6},{6,4},{8,10},{10,8},{12,14},{14,12},{16,18},{18,... | collective-permute-start | bytes 393224 | tf_op jit(solution)/shard_map/ppermute | solution.py:18
  590.2 1237.6 %collective-permute-start.17 = (bf16[64,8,128]{2,0,1:T(8,128)(2,1)S(1)}, bf16[64,8,128]{2,0,1:T(8,128)(2,1)S(1)}, u32[]{:S(2)}, u32[]{:S(2)}) collective-permute-start(bf16[64,8,128]{2,0,1:T(8,128)(2,1)S(1)} %fusion.48), channel_id=1, source_target_pairs={{0,2},{2,0},{4,6},{6,4},{8,10},{10,8},{12,14},{14,12},{16,18},{18,... | collective-permute-start | bytes 393224 | tf_op jit(solution)/shard_map/ppermute | solution.py:18
  1822.9 9.1 all-to-all-start.3
  1832.1 9.6 all-to-all-start.7
  1841.7 8.3 all-to-all-start.6
  (213 other events, 347.9 us)
Sparse Core Ops, SparseCore 0:
  558.1 1259.7 all-reduce.4
where the time goes:
time: 1870 us; the launch traced here: 1860 us
  waiting for transfers between devices  1250 us (67%)
  blocking collectives  360 us (19%)
  local copies, waits for them, and re-layouts  123 us (7%)
  starting transfers between devices  70.7 us (4%)
  other arithmetic  24.6 us (1%)
    unnamed x2, waiting for transfers between devices  1230 us
    all_gather x1, blocking collectives, local(): lax.all_gather(key_pool[level_count], 'seq', axis=0, tiled=True)  184 us
    all_gather x1, blocking collectives, local(): lax.all_gather(value_pool[level_count], 'seq', axis=0, tiled=True)  176 us
  transfers between devices with their start and end apart: 33, of which 13 were waited for; matrix products, arithmetic and copies ran while one was open for 6% of the time, Pallas kernels for 0%

commit v1 on v0

--- a/solution.py
+++ b/solution.py
@@ -63,7 +63,12 @@
             sib_keys, sib_values = swapped((own_keys, own_values), "seq", level_no - 1)
         else:
             whole_keys, whole_values = (
-                lax.all_gather(key_pool[level_count], "seq", axis=0, tiled=True),
+                jnp.concatenate(
+                    lax.all_to_all(
+                        jnp.stack([key_pool[level_count]] * lax.axis_size("seq")), "seq", 0, 0
+                    ),
+                    axis=0,
+                ),
                 lax.all_gather(value_pool[level_count], "seq", axis=0, tiled=True),
             )
             sib_keys = lax.dynamic_slice_in_dim(whole_keys, sibling_start, half_rows, 0)

time: 1870 us -> 1730 us (0.925)
  blocking collectives: 360 us -> 194 us
    all_gather x1 -> x0, blocking collectives: 184 us -> none  [local(): lax.all_gather(key_pool[level_count], 'seq', axis=0, tiled=True)]
  transfers between devices with their start and end apart: 33 -> 34, of which waited for: 13 -> 12; matrix products, arithmetic and copies ran while one was open for 6% -> 7% of each run, Pallas kernels for 0% -> 0%
where the time goes in v1:
time: 1730 us; the launch traced here: 1720 us
  waiting for transfers between devices  1250 us (72%)
  blocking collectives  194 us (11%)
  local copies, waits for them, and re-layouts  123 us (7%)
  starting transfers between devices  82.5 us (5%)
  other arithmetic  25.4 us (1%)
  matrix products  19.8 us (1%)
    unnamed x2, waiting for transfers between devices  1230 us
    all_gather x1, blocking collectives, local(): lax.all_gather(value_pool[level_count], 'seq', axis=0, tiled=True)  194 us
  transfers between devices with their start and end apart: 34, of which 12 were waited for; matrix products, arithmetic and copies ran while one was open for 7% of the time, Pallas kernels for 0%

profile of v1, /device:TPU:8, one launch (start us, length us, event | category | flops | bytes accessed | tf_op | source)
XLA Modules:
  0.0 1716.3 jit_solution(79401301146423357)
XLA Ops:
  7.2 1.7 copy.2301
  8.8 5.7 all-to-all-start.1
  18.7 4.5 all-to-all-start.3
  26.4 5.4 all-to-all-start
  32.8 2.1 all-to-all-done
  35.0 5.4 all-to-all-start.5
  43.6 194.4 %all-gather = bf16[128,1,8,128]{3,2,1,0:T(8,128)(2,1)} all-gather(bf16[1,1,8,128]{3,2,1,0:T(8,128)(2,1)S(1)} %fusion.260), channel_id=2, replica_groups=mesh['seq'=128,'head'=2] {'seq'}, dimensions={0}, use_global_device_ids=true | all-gather | bytes 264192 | tf_op jit(solution)/shard_map/all_gather | solution.py:72
  241.0 7.3 all-to-all-start.2
  268.5 3.0 collective-permute-start.2
  293.5 2.5 collective-permute-start.3
  327.6 2.2 collective-permute-start.5
  346.5 1.4 fusion.282
  349.3 3.7 multiply_reduce_fusion.4
  353.8 1.4 reduce_sum.256
  357.9 1.4 reduce_sum.252
  368.4 2.1 collective-permute-start.18
  398.3 6.9 all-to-all-start.6
  410.3 1.5 collective-permute-start.19
  414.7 1.6 collective-permute-done.19
  417.5 2.2 collective-permute-start.20
  420.9 1.9 collective-permute-start.14
  425.3 3.1 collective-permute-start.21
  429.6 2.1 collective-permute-start.15
  434.6 2.7 collective-permute-done.15
  439.2 3.7 collective-permute-done.16
  443.4 1232.9 %all-reduce.5.cloned.1.call-done = (f32[128,8,128]{2,1,0:T(8,128)}, f32[128,8,128]{2,1,0:T(8,128)}) async-done(((f32[128,8,128]{2,1,0:T(8,128)}, f32[128,8,128]{2,1,0:T(8,128)}), (f32[128,8,128]{2,1,0:T(8,128)}, f32[128,8,128]{2,1,0:T(8,128)})) %all-reduce.5.cloned.1.call-update) | async-done | bytes 1048592
  1681.4 4.9 all-to-all-start.4
  1686.4 4.1 all-to-all-done.4
  1690.5 5.6 all-to-all-start.8
  1697.6 2.6 all-to-all-done.8
  1700.1 5.2 all-to-all-start.7
  1705.3 1.7 copy.1943
  (887 shorter events, 172.0 us)
Async XLA Ops:
  8.8 9.9 all-to-all-start.1
  18.7 7.7 all-to-all-start.3
  26.4 8.6 all-to-all-start
  32.1 220.6 %collective-permute-start.6 = (bf16[64,8,128]{2,0,1:T(8,128)(2,1)S(1)}, bf16[64,8,128]{2,0,1:T(8,128)(2,1)S(1)}, u32[]{:S(2)}, u32[]{:S(2)}) collective-permute-start(bf16[64,8,128]{2,0,1:T(8,128)(2,1)S(1)} %bitcast.782), channel_id=1, source_target_pairs={{0,2},{2,0},{4,6},{6,4},{8,10},{10,8},{12,14},{14,12},{16,18},{18,... | collective-permute-start | bytes 393224 | tf_op jit(solution)/shard_map/ppermute | solution.py:18
  35.0 8.6 all-to-all-start.5
  40.7 212.0 %collective-permute-start = (bf16[64,8,128]{2,0,1:T(8,128)(2,1)S(1)}, bf16[64,8,128]{2,0,1:T(8,128)(2,1)S(1)}, u32[]{:S(2)}, u32[]{:S(2)}) collective-permute-start(bf16[64,8,128]{2,0,1:T(8,128)(2,1)S(1)} %bitcast.784), channel_id=1, source_target_pairs={{0,2},{2,0},{4,6},{6,4},{8,10},{10,8},{12,14},{14,12},{16,18},{18,... | collective-permute-start | bytes 393224 | tf_op jit(solution)/shard_map/ppermute | solution.py:18
  241.0 62.1 %all-to-all-start.2 = ((bf16[128,1,8,128]{3,2,1,0:T(8,128)(2,1)}), bf16[128,1,8,128]{3,2,1,0:T(8,128)(2,1)}, u32[]{:S(2)}, u32[]{:S(2)}) async-start(bf16[128,1,8,128]{3,2,1,0:T(8,128)(2,1)} %stack.5), calls=%async_computation.2 | async-start | bytes 524288 | tf_op jit(solution)/shard_map/all_to_all | solution.py:67
  254.0 13.9 collective-permute-start.1
  259.2 15.5 collective-permute-start.7
  268.5 16.9 collective-permute-start.2
  276.9 19.2 %collective-permute-start.8 = (bf16[64,8,128]{2,0,1:T(8,128)(2,1)}, bf16[64,8,128]{2,0,1:T(8,128)(2,1)S(1)}, u32[]{:S(2)}, u32[]{:S(2)}) collective-permute-start(bf16[64,8,128]{2,0,1:T(8,128)(2,1)} %fusion.136), channel_id=1, source_target_pairs={{0,8},{8,0},{2,10},{10,2},{4,12},{12,4},{6,14},{14,6},{16,24},{24,... | collective-permute-start | bytes 393224 | tf_op jit(solution)/shard_map/ppermute | solution.py:18
  293.5 12.3 collective-permute-start.3
  299.3 15.5 collective-permute-start.9
  313.6 8.8 collective-permute-start.4
  317.2 12.6 collective-permute-start.10
  327.6 11.3 collective-permute-start.5
  333.6 9.7 collective-permute-start.11
  368.4 39.9 %collective-permute-start.18 = (bf16[64,8,128]{2,0,1:T(8,128)(2,1)}, bf16[64,8,128]{2,0,1:T(8,128)(2,1)}, u32[]{:S(2)}, u32[]{:S(2)}) collective-permute-start(bf16[64,8,128]{2,0,1:T(8,128)(2,1)} %fusion.60), channel_id=1, source_target_pairs={{0,64},{64,0},{2,66},{66,2},{4,68},{68,4},{6,70},{70,6},{8,72},{72... | collective-permute-start | bytes 393224 | tf_op jit(solution)/shard_map/ppermute | solution.py:18
  384.0 27.9 %collective-permute-start.12 = (bf16[64,8,128]{2,0,1:T(8,128)(2,1)}, bf16[64,8,128]{2,0,1:T(8,128)(2,1)}, u32[]{:S(2)}, u32[]{:S(2)}) collective-permute-start(bf16[64,8,128]{2,0,1:T(8,128)(2,1)} %fusion.53), channel_id=1, source_target_pairs={{0,64},{64,0},{2,66},{66,2},{4,68},{68,4},{6,70},{70,6},{8,72},{72... | collective-permute-start | bytes 393224 | tf_op jit(solution)/shard_map/ppermute | solution.py:18
  398.3 1283.0 %all-to-all-start.6 = ((bf16[2,64,1024]{2,1,0:T(8,128)(2,1)}), bf16[2,64,1024]{2,1,0:T(8,128)(2,1)}, u32[]{:S(2)}, u32[]{:S(2)}) async-start(bf16[2,64,1024]{2,1,0:T(8,128)(2,1)} %all_to_all.124), calls=%async_computation.6 | async-start | bytes 524288 | tf_op jit(solution)/shard_map/all_to_all | solution.py:239
  405.2 1271.1 %all-reduce.5.cloned.1.call-start = ((), (), s32[]{:S(2)}) async-start(), calls=%async_computation.9 | async-start | bytes 2097152
  410.3 5.9 collective-permute-start.19
  413.8 6.0 collective-permute-start.13
  417.5 6.6 collective-permute-start.20
  420.9 7.5 collective-permute-start.14
  425.3 7.7 collective-permute-start.21
  429.6 7.8 collective-permute-start.15
  439.1 1238.6 %collective-permute-start.23 = (bf16[64,8,128]{2,0,1:T(8,128)(2,1)S(1)}, bf16[64,8,128]{2,0,1:T(8,128)(2,1)S(1)}, u32[]{:S(2)}, u32[]{:S(2)}) collective-permute-start(bf16[64,8,128]{2,0,1:T(8,128)(2,1)S(1)} %fusion.46), channel_id=1, source_target_pairs={{0,2},{2,0},{4,6},{6,4},{8,10},{10,8},{12,14},{14,12},{16,18},{18,... | collective-permute-start | bytes 393224 | tf_op jit(solution)/shard_map/ppermute | solution.py:18
  443.3 1242.9 %collective-permute-start.17 = (bf16[64,8,128]{2,0,1:T(8,128)(2,1)S(1)}, bf16[64,8,128]{2,0,1:T(8,128)(2,1)S(1)}, u32[]{:S(2)}, u32[]{:S(2)}) collective-permute-start(bf16[64,8,128]{2,0,1:T(8,128)(2,1)S(1)} %fusion.48), channel_id=1, source_target_pairs={{0,2},{2,0},{4,6},{6,4},{8,10},{10,8},{12,14},{14,12},{16,18},{18,... | collective-permute-start | bytes 393224 | tf_op jit(solution)/shard_map/ppermute | solution.py:18
  1681.4 9.1 all-to-all-start.4
  1690.5 9.6 all-to-all-start.8
  1700.1 8.3 all-to-all-start.7
  (212 other events, 529.3 us)
Sparse Core Ops, SparseCore 0:
  408.6 1267.6 all-reduce.4
